TPU v7x, 128 devices: a whole 4x4x4 slice. The times are simulated.
128 devices in a mesh: row: 16 (over z_lo, y, core), col: 8 (over z_hi, x).
Axes of the slice: x: 4, y: 4, z: 4 (z_hi: 2, z_lo: 2; z = z_hi * 2 + z_lo), core: 2. Of those that a mesh axis runs over, the one named last changes fastest.
Arguments:
- a_values: float32 [8192, 8192], P('row', 'col'), may hold values from -6 to 6
- a_mask: int32 [64, 64], P('row', 'col'), may hold values from 0 to 1, as said below
- b_values: float32 [8192, 8192], P('row', 'col'), may hold values from -0.5 to 0.5
- b_mask: int32 [64, 64], P('row', 'col'), may hold values from 0 to 1, as said below
- keep: int32 [64, 64, 64], P('row', None, 'col'), may hold values from 0 to 1, as said below
Outputs:
- product: float32 [8192, 8192], P('row', 'col')
Inputs may be any that keep to these rules, and one draw needn't show every extreme that they name: `keep`: 0 means the triple is filtered out, 1 that it counts. `a_mask`: 1 means the block is stored; on one device at most 20 blocks are stored, and some device holds exactly 20. `b_mask`: 1 means the block is stored; on one device at most 20 blocks are stored, and some device holds exactly 20.
All inputs are finite; a program needn't handle non-finite values.
Results may differ from a plain program's by a relative error of at most 0.000071.
Values sent between devices are 32-bit elements; how exact they have to be, the bound alone decides.
No kernel may reach another device: no remote copies, remote signals or barrier semaphores. Data moves between devices by JAX's collectives and lax.ppermute only.
A program may use at most 384 MiB of HBM per device.

v0:
```python
import jax
import jax.numpy as jnp
from jax import lax
from jax.sharding import PartitionSpec as P


def per_device(a_values, a_mask, b_values, b_mask, keep):
    row_blocks, inner_local = a_mask.shape
    inner_rows, col_blocks = b_mask.shape
    width = a_values.shape[0] // row_blocks
    first = (
        a_values.reshape(row_blocks, width, inner_local, width)
        * a_mask.astype(jnp.float32)[:, None, :, None]
    ).reshape(a_values.shape)
    first_whole = lax.all_gather(first, "col", axis=1, tiled=True)
    second = (
        b_values.reshape(inner_rows, width, col_blocks, width)
        * b_mask.astype(jnp.float32)[:, None, :, None]
    ).reshape(b_values.shape)
    weights = jnp.repeat(keep.astype(jnp.float32), width, axis=1)
    piece = lax.all_gather(second, "row", axis=0, tiled=True)
    count = piece.shape[0]
    shaped = first_whole.reshape(row_blocks, width, count)
    results = []
    for column in range(col_blocks):
        masked = (shaped * weights[:, None, :, column]).reshape(row_blocks * width, count)
        results.append(
            jnp.dot(
                masked,
                piece[:, column * width : (column + 1) * width],
                precision=lax.Precision.HIGHEST,
                preferred_element_type=jnp.float32,
            )
        )
    return jnp.concatenate(results, axis=1)


def solution(mesh):
    return jax.shard_map(
        per_device,
        mesh=mesh,
        in_specs=(
            P("row", "col"),
            P("row", "col"),
            P("row", "col"),
            P("row", "col"),
            P("row", None, "col"),
        ),
        out_specs=P("row", "col"),
        check_vma=False,
    )
```

profile of v0, /device:TPU:1, one launch (start us, length us, event | category | flops | bytes accessed | tf_op | source)
XLA Modules:
  0.0 541.8 jit_solution(7089609412667732679)
XLA Ops:
  6.5 0.0 copy-start.1
  6.5 0.0 all-gather.3.cloned.1.call-start
  6.5 0.7 convert_element_type.9
  7.2 0.2 mul.126
  7.4 3.6 bitcast_multiply_fusion.9
  11.1 0.0 all-gather.3.cloned.1.call-update
  11.1 0.0 all-gather.5.cloned.1.call-start
  11.1 0.7 convert_element_type.11
  11.8 0.2 mul.133
  12.0 3.6 bitcast_multiply_fusion.8
  15.6 0.0 all-gather.5.cloned.1.call-update
  15.7 0.0 copy-done.1
  15.7 0.3 broadcast_in_dim.2
  16.0 0.4 reshape.36
  16.5 0.1 slice_bitcast_fusion
  16.5 183.4 %all-gather.3.cloned.1.call-done = f32[512,8192]{1,0:T(8,128)} async-done(((f32[512,1024]{1,0:T(8,128)}), f32[512,8192]{1,0:T(8,128)}) %all-gather.3.cloned.1.call-update) | async-done | bytes 16777232 | tf_op jit(solution)/shard_map/all_gather | solution.py:15
  200.0 51.5 %bitcast_multiply_fusion = (f32[512,8192]{1,0:T(8,128)}, f32[512,8192]{1,0:T(8,128)}, f32[512,8192]{1,0:T(8,128)}, f32[512,8192]{1,0:T(8,128)}, f32[512,8192]{1,...) fusion(f32[512,8192]{1,0:T(8,128)} %all-gather.3.cloned.1.call-done, ...), kind=kLoop, calls=%fused_computation | loop fusion | flops 33554432 | bytes 152043520 | tf_op jit(solution)/shard_map/mul | solution.py:26
  251.4 119.5 %all-gather.5.cloned.1.call-done = f32[8192,1024]{1,0:T(8,128)} async-done(((f32[512,1024]{1,0:T(8,128)}), f32[8192,1024]{1,0:T(8,128)}) %all-gather.5.cloned.1.call-update) | async-done | bytes 33554448 | tf_op jit(solution)/shard_map/all_gather | solution.py:21
  370.9 0.0 copy-start
  370.9 18.5 %fusion.16 = f32[512,1024]{0,1:T(8,128)S(1)} fusion(f32[512,8192]{1,0:T(8,128)} %get-tuple-element.12, f32[8192,1024]{1,0:T(8,128)} %all-gather.5.cloned.1.call-done), kind=kOutput, calls=%fused_computation.26 | convolution fusion | flops 6442450944 | bytes 21233664 | tf_op jit(solution)/shard_map/dot_general | solution.py:28
  389.4 0.0 copy-done
  389.4 30.7 %fusion.19 = f32[512,1024]{0,1:T(8,128)S(1)} fusion(f32[512,1024]{0,1:T(8,128)S(1)} %fusion.16, f32[512,8192]{1,0:T(8,128)S(1)} %copy-done, f32[8192,1024]{1,0:T(8,128)} %all-gather.5.cloned.1.call-done), kind=kOutput, calls=%fused_computation.27 | convolution fusion | flops 6442450944 | bytes 21233664 | tf_op jit(solution)/shard_map/dot_general | solution.py:28
  420.1 0.0 slice-start.4
  420.1 0.0 slice-start.5
  420.1 18.2 %fusion.22 = f32[512,1024]{0,1:T(8,128)S(1)} fusion(f32[512,1024]{0,1:T(8,128)S(1)} %fusion.19, f32[512,8192]{1,0:T(8,128)} %get-tuple-element.10, f32[8192,1024]{1,0:T(8,128)} %all-gather.5.cloned.1.call-done), kind=kOutput, calls=%fused_computation.28 | convolution fusion | flops 6442450944 | bytes 21233664 | tf_op jit(solution)/shard_map/dot_general | solution.py:28
  438.3 0.0 slice-start.6
  438.3 0.0 slice-start.7
  438.3 18.6 %fusion.25 = f32[512,1024]{0,1:T(8,128)S(1)} fusion(f32[512,1024]{0,1:T(8,128)S(1)} %fusion.22, f32[512,8192]{1,0:T(8,128)} %get-tuple-element.9, f32[8192,1024]{1,0:T(8,128)} %all-gather.5.cloned.1.call-done), kind=kOutput, calls=%fused_computation.29 | convolution fusion | flops 6442450944 | bytes 21233664 | tf_op jit(solution)/shard_map/dot_general | solution.py:28
  456.9 0.0 slice-done.4
  456.9 0.0 slice-done.5
  456.9 0.0 slice-done.6
  456.9 0.0 slice-done.7
  456.9 19.7 %fusion.28 = f32[512,1024]{0,1:T(8,128)S(1)} fusion(f32[512,1024]{0,1:T(8,128)S(1)} %fusion.25, f32[512,8192]{1,0:T(8,128)S(1)} %bitcast.55, f32[8192,1024]{1,0:T(8,128)} %all-gather.5.cloned.1.call-done), kind=kOutput, calls=%fused_computation.30 | convolution fusion | flops 6442450944 | bytes 21233664 | tf_op jit(solution)/shard_map/dot_general | solution.py:28
  476.6 0.0 slice-start
  476.6 0.0 slice-start.1
  476.6 18.2 %fusion.31 = f32[512,1024]{0,1:T(8,128)S(1)} fusion(f32[512,1024]{0,1:T(8,128)S(1)} %fusion.28, f32[512,8192]{1,0:T(8,128)} %get-tuple-element.7, f32[8192,1024]{1,0:T(8,128)} %all-gather.5.cloned.1.call-done), kind=kOutput, calls=%fused_computation.31 | convolution fusion | flops 6442450944 | bytes 21233664 | tf_op jit(solution)/shard_map/dot_general | solution.py:28
  494.8 0.0 slice-start.2
  494.8 0.0 slice-start.3
  494.8 18.4 %fusion.34 = f32[512,1024]{0,1:T(8,128)S(1)} fusion(f32[512,1024]{0,1:T(8,128)S(1)} %fusion.31, f32[512,8192]{1,0:T(8,128)} %get-tuple-element.6, f32[8192,1024]{1,0:T(8,128)} %all-gather.5.cloned.1.call-done), kind=kOutput, calls=%fused_computation.32 | convolution fusion | flops 6442450944 | bytes 21233664 | tf_op jit(solution)/shard_map/dot_general | solution.py:28
  513.2 0.0 slice-done
  513.2 0.0 slice-done.1
  513.2 0.0 slice-done.2
  513.3 0.0 slice-done.3
  513.3 19.5 %fusion.37 = f32[512,1024]{0,1:T(8,128)S(1)} fusion(f32[512,1024]{0,1:T(8,128)S(1)} %fusion.34, f32[512,8192]{1,0:T(8,128)S(1)} %bitcast.53, f32[8192,1024]{1,0:T(8,128)} %all-gather.5.cloned.1.call-done), kind=kOutput, calls=%fused_computation.33 | convolution fusion | flops 6442450944 | bytes 21233664 | tf_op jit(solution)/shard_map/dot_general | solution.py:28
  532.8 1.8 copy.7
  (4 shorter events, 0.0 us)
Async XLA Ops:
  6.5 9.1 %copy-start.1 = (s32[4,64,8]{1,2,0:T(8,128)S(1)}, s32[4,64,8]{1,2,0:T(8,128)}, u32[]{:S(2)}) copy-start(s32[4,64,8]{1,2,0:T(8,128)} %param.9) | copy-start | bytes 24580
  6.5 193.4 %all-gather.3.cloned.1.call-start = ((), (), s32[]{:S(2)}) async-start(), calls=%async_computation | async-start | bytes 18874368 | tf_op jit(solution)/shard_map/all_gather | solution.py:15
  11.1 359.8 %all-gather.5.cloned.1.call-start = ((), (), s32[]{:S(2)}) async-start(), calls=%async_computation.1 | async-start | bytes 35651584 | tf_op jit(solution)/shard_map/all_gather | solution.py:21
  370.9 18.5 %copy-start = (f32[512,8192]{1,0:T(8,128)S(1)}, f32[512,8192]{1,0:T(8,128)}, u32[]{:S(2)}) copy-start(f32[512,8192]{1,0:T(8,128)} %get-tuple-element.11) | copy-start | bytes 50331652
  420.1 36.8 %slice-start.4 = ((s8[16777216]{0:T(1024)(128)(4,1)}), s8[4194304]{0:T(1024)(128)(4,1)S(1)}, s32[]{:S(2)}) async-start(s8[16777216]{0:T(1024)(128)(4,1)} %bitcast.54), calls=%async_computation.6 | async-start | bytes 8388608
  420.1 36.8 %slice-start.5 = ((s8[16777216]{0:T(1024)(128)(4,1)}), s8[4194304]{0:T(1024)(128)(4,1)S(1)}, s32[]{:S(2)}) async-start(s8[16777216]{0:T(1024)(128)(4,1)} %bitcast.54), calls=%async_computation.7 | async-start | bytes 8388608
  438.3 18.6 %slice-start.6 = ((s8[16777216]{0:T(1024)(128)(4,1)}), s8[4194304]{0:T(1024)(128)(4,1)S(1)}, s32[]{:S(2)}) async-start(s8[16777216]{0:T(1024)(128)(4,1)} %bitcast.54), calls=%async_computation.8 | async-start | bytes 8388608
  438.3 18.6 %slice-start.7 = ((s8[16777216]{0:T(1024)(128)(4,1)}), s8[4194304]{0:T(1024)(128)(4,1)S(1)}, s32[]{:S(2)}) async-start(s8[16777216]{0:T(1024)(128)(4,1)} %bitcast.54), calls=%async_computation.9 | async-start | bytes 8388608
  476.6 36.6 %slice-start = ((s8[16777216]{0:T(1024)(128)(4,1)}), s8[4194304]{0:T(1024)(128)(4,1)S(1)}, s32[]{:S(2)}) async-start(s8[16777216]{0:T(1024)(128)(4,1)} %bitcast.52), calls=%async_computation.2 | async-start | bytes 8388608
  476.6 36.6 %slice-start.1 = ((s8[16777216]{0:T(1024)(128)(4,1)}), s8[4194304]{0:T(1024)(128)(4,1)S(1)}, s32[]{:S(2)}) async-start(s8[16777216]{0:T(1024)(128)(4,1)} %bitcast.52), calls=%async_computation.3 | async-start | bytes 8388608
  494.8 18.4 %slice-start.2 = ((s8[16777216]{0:T(1024)(128)(4,1)}), s8[4194304]{0:T(1024)(128)(4,1)S(1)}, s32[]{:S(2)}) async-start(s8[16777216]{0:T(1024)(128)(4,1)} %bitcast.52), calls=%async_computation.4 | async-start | bytes 8388608
  494.8 18.4 %slice-start.3 = ((s8[16777216]{0:T(1024)(128)(4,1)}), s8[4194304]{0:T(1024)(128)(4,1)S(1)}, s32[]{:S(2)}) async-start(s8[16777216]{0:T(1024)(128)(4,1)} %bitcast.52), calls=%async_computation.5 | async-start | bytes 8388608
Sparse Core Ops, SparseCore 0:
  11.2 188.7 all-gather.2
  201.7 169.1 all-gather.4
where the time goes:
time: 550 us; the launch traced here: 542 us
  waiting for transfers between devices  303 us (55%)
  matrix products  162 us (29%)
  other arithmetic  60.1 us (11%)
  between operations  14.1 us (3%)
    all_gather x1, waiting for transfers between devices, per_device(): first_whole = lax.all_gather(first, 'col', axis=1, tiled=True)  183 us
    dot_general x8, matrix products, per_device(): jnp.dot(masked, piece[:, column * width:(column + 1) * width], precision=...  162 us
    all_gather x1, waiting for transfers between devices, per_device(): piece = lax.all_gather(second, 'row', axis=0, tiled=True)  119 us
    mul x1, other arithmetic, per_device(): shaped * weights[:, None, :, column]  51.5 us
  transfers between devices with their start and end apart: 2, of which 2 were waited for; matrix products, arithmetic and copies ran while one was open for 10% of the time, Pallas kernels for 0%

commit v1 on v0

--- a/solution.py
+++ b/solution.py
@@ -18,7 +18,9 @@
         * b_mask.astype(jnp.float32)[:, None, :, None]
     ).reshape(b_values.shape)
     weights = jnp.repeat(keep.astype(jnp.float32), width, axis=1)
-    piece = lax.all_gather(second, "row", axis=0, tiled=True)
+    piece = jnp.concatenate(
+        lax.all_to_all(jnp.stack([second] * lax.axis_size("row")), "row", 0, 0), axis=0
+    )
     count = piece.shape[0]
     shaped = first_whole.reshape(row_blocks, width, count)
     results = []

time: 550 us -> 765 us (1.39)
  waiting for transfers between devices: 303 us -> 506 us
  local copies, waits for them, and re-layouts: 3.08 us -> 14.4 us
    all_gather x1, waiting for transfers between devices: 183 us -> 506 us  [per_device(): first_whole = lax.all_gather(first, 'col', axis=1, tiled=True)]
    all_gather x1 -> x0, waiting for transfers between devices: 119 us -> none  [per_device(): piece = lax.all_gather(second, 'row', axis=0, tiled=True)]
    another operation x0 -> x1, local copies, waits for them, and re-layouts: none -> 11.4 us  [per_device(): jnp.stack([second] * lax.axis_size('row'))]
  transfers between devices with their start and end apart: 2 -> 2, of which waited for: 2 -> 1; matrix products, arithmetic and copies ran while one was open for 10% -> 7% of each run, Pallas kernels for 0% -> 0%
where the time goes in v1:
time: 765 us; the launch traced here: 756 us
  waiting for transfers between devices  506 us (66%)
  matrix products  162 us (21%)
  other arithmetic  53 us (7%)
  local copies, waits for them, and re-layouts  14.4 us (2%)
  between operations  14.1 us (2%)
    all_gather x1, waiting for transfers between devices, per_device(): first_whole = lax.all_gather(first, 'col', axis=1, tiled=True)  506 us
    dot_general x8, matrix products, per_device(): jnp.dot(masked, piece[:, column * width:(column + 1) * width], precision=...  162 us
    mul x1, other arithmetic, per_device(): shaped * weights[:, None, :, column]  47.9 us
  transfers between devices with their start and end apart: 2, of which 1 were waited for; matrix products, arithmetic and copies ran while one was open for 7% of the time, Pallas kernels for 0%

profile of v1, /device:TPU:1, one launch (start us, length us, event | category | flops | bytes accessed | tf_op | source)
XLA Modules:
  0.0 756.5 jit_solution(15369945244902268368)
XLA Ops:
  6.5 0.7 convert_element_type.11
  7.2 0.2 mul.134
  7.4 2.3 bitcast_multiply_fusion.8
  9.7 11.4 %stack.3 = f32[16,512,1024]{2,1,0:T(8,128)} broadcast(f32[512,1024]{1,0:T(8,128)S(1)} %bitcast_multiply_fusion.8), dimensions={1,2} | broadcast | bytes 35651584 | tf_op jit(solution)/shard_map/stack | solution.py:22
  21.1 0.0 copy-start.3
  21.1 0.0 copy-start.1
  21.1 0.0 copy-start.2
  21.1 7.5 all-to-all-start
  28.6 0.0 all-gather.2.cloned.1.call-start
  28.6 0.0 copy-done.3
  28.6 0.2 mul.127
  28.9 0.0 copy-done.1
  28.9 2.0 bitcast_multiply_fusion.9
  30.9 0.0 all-gather.2.cloned.1.call-update
  30.9 0.0 copy-done.2
  31.0 0.3 broadcast_in_dim.2
  31.3 0.4 reshape.41
  31.7 0.1 slice_bitcast_fusion
  31.8 505.8 %all-gather.2.cloned.1.call-done = f32[512,8192]{1,0:T(8,128)} async-done(((f32[512,1024]{1,0:T(8,128)}), f32[512,8192]{1,0:T(8,128)}) %all-gather.2.cloned.1.call-update) | async-done | bytes 16777232 | tf_op jit(solution)/shard_map/all_gather | solution.py:15
  537.6 47.9 %bitcast_multiply_fusion = (f32[512,8192]{1,0:T(8,128)}, f32[512,8192]{1,0:T(8,128)}, f32[512,8192]{1,0:T(8,128)}, f32[512,8192]{1,0:T(8,128)}, f32[512,8192]{1,...) fusion(f32[512,8192]{1,0:T(8,128)} %all-gather.2.cloned.1.call-done, ...), kind=kLoop, calls=%fused_computation | loop fusion | flops 33554432 | bytes 152043520 | tf_op jit(solution)/shard_map/mul | solution.py:28
  585.5 0.0 all-to-all-done
  585.5 0.0 copy-start
  585.5 18.5 %fusion.16 = f32[512,1024]{0,1:T(8,128)S(1)} fusion(f32[512,8192]{1,0:T(8,128)} %get-tuple-element.12, f32[8192,1024]{1,0:T(8,128)} %bitcast.2), kind=kOutput, calls=%fused_computation.26 | convolution fusion | flops 6442450944 | bytes 21233664 | tf_op jit(solution)/shard_map/dot_general | solution.py:30
  604.0 0.0 copy-done
  604.0 30.7 %fusion.19 = f32[512,1024]{0,1:T(8,128)S(1)} fusion(f32[512,1024]{0,1:T(8,128)S(1)} %fusion.16, f32[512,8192]{1,0:T(8,128)S(1)} %copy-done, f32[8192,1024]{1,0:T(8,128)} %bitcast.2), kind=kOutput, calls=%fused_computation.27 | convolution fusion | flops 6442450944 | bytes 21233664 | tf_op jit(solution)/shard_map/dot_general | solution.py:30
  634.7 0.0 slice-start.4
  634.7 0.0 slice-start.5
  634.7 18.2 %fusion.22 = f32[512,1024]{0,1:T(8,128)S(1)} fusion(f32[512,1024]{0,1:T(8,128)S(1)} %fusion.19, f32[512,8192]{1,0:T(8,128)} %get-tuple-element.10, f32[8192,1024]{1,0:T(8,128)} %bitcast.2), kind=kOutput, calls=%fused_computation.28 | convolution fusion | flops 6442450944 | bytes 21233664 | tf_op jit(solution)/shard_map/dot_general | solution.py:30
  652.9 0.0 slice-start.6
  652.9 0.0 slice-start.7
  652.9 18.6 %fusion.25 = f32[512,1024]{0,1:T(8,128)S(1)} fusion(f32[512,1024]{0,1:T(8,128)S(1)} %fusion.22, f32[512,8192]{1,0:T(8,128)} %get-tuple-element.9, f32[8192,1024]{1,0:T(8,128)} %bitcast.2), kind=kOutput, calls=%fused_computation.29 | convolution fusion | flops 6442450944 | bytes 21233664 | tf_op jit(solution)/shard_map/dot_general | solution.py:30
  671.5 0.0 slice-done.4
  671.5 0.0 slice-done.5
  671.5 0.0 slice-done.6
  671.5 0.0 slice-done.7
  671.6 19.7 %fusion.28 = f32[512,1024]{0,1:T(8,128)S(1)} fusion(f32[512,1024]{0,1:T(8,128)S(1)} %fusion.25, f32[512,8192]{1,0:T(8,128)S(1)} %bitcast.56, f32[8192,1024]{1,0:T(8,128)} %bitcast.2), kind=kOutput, calls=%fused_computation.30 | convolution fusion | flops 6442450944 | bytes 21233664 | tf_op jit(solution)/shard_map/dot_general | solution.py:30
  691.2 0.0 slice-start
  691.2 0.0 slice-start.1
  691.3 18.2 %fusion.31 = f32[512,1024]{0,1:T(8,128)S(1)} fusion(f32[512,1024]{0,1:T(8,128)S(1)} %fusion.28, f32[512,8192]{1,0:T(8,128)} %get-tuple-element.7, f32[8192,1024]{1,0:T(8,128)} %bitcast.2), kind=kOutput, calls=%fused_computation.31 | convolution fusion | flops 6442450944 | bytes 21233664 | tf_op jit(solution)/shard_map/dot_general | solution.py:30
  709.4 0.0 slice-start.2
  709.5 0.0 slice-start.3
  709.5 18.4 %fusion.34 = f32[512,1024]{0,1:T(8,128)S(1)} fusion(f32[512,1024]{0,1:T(8,128)S(1)} %fusion.31, f32[512,8192]{1,0:T(8,128)} %get-tuple-element.6, f32[8192,1024]{1,0:T(8,128)} %bitcast.2), kind=kOutput, calls=%fused_computation.32 | convolution fusion | flops 6442450944 | bytes 21233664 | tf_op jit(solution)/shard_map/dot_general | solution.py:30
  727.9 0.0 slice-done
  727.9 0.0 slice-done.1
  727.9 0.0 slice-done.2
  727.9 0.0 slice-done.3
  727.9 19.5 %fusion.37 = f32[512,1024]{0,1:T(8,128)S(1)} fusion(f32[512,1024]{0,1:T(8,128)S(1)} %fusion.34, f32[512,8192]{1,0:T(8,128)S(1)} %bitcast.54, f32[8192,1024]{1,0:T(8,128)} %bitcast.2), kind=kOutput, calls=%fused_computation.33 | convolution fusion | flops 6442450944 | bytes 21233664 | tf_op jit(solution)/shard_map/dot_general | solution.py:30
  747.4 1.8 copy.7
  (5 shorter events, 0.0 us)
Async XLA Ops:
  21.1 7.5 copy-start.3
  21.1 7.8 %copy-start.1 = (f32[512,1024]{1,0:T(8,128)S(1)}, f32[512,1024]{1,0:T(8,128)}, u32[]{:S(2)}) copy-start(f32[512,1024]{1,0:T(8,128)} %param.5) | copy-start | bytes 6291460
  21.1 9.8 %copy-start.2 = (s32[4,64,8]{1,2,0:T(8,128)S(1)}, s32[4,64,8]{1,2,0:T(8,128)}, u32[]{:S(2)}) copy-start(s32[4,64,8]{1,2,0:T(8,128)} %param.9) | copy-start | bytes 24580
  21.1 564.4 %all-to-all-start = ((f32[16,512,1024]{2,1,0:T(8,128)}), f32[16,512,1024]{2,1,0:T(8,128)}, u32[]{:S(2)}, u32[]{:S(2)}) async-start(f32[16,512,1024]{2,1,0:T(8,128)} %stack.3), calls=%async_computation | async-start | bytes 67108864 | tf_op jit(solution)/shard_map/all_to_all | solution.py:22
  28.6 509.0 %all-gather.2.cloned.1.call-start = ((), (), s32[]{:S(2)}) async-start(), calls=%async_computation.1 | async-start | bytes 18874368 | tf_op jit(solution)/shard_map/all_gather | solution.py:15
  585.5 18.5 %copy-start = (f32[512,8192]{1,0:T(8,128)S(1)}, f32[512,8192]{1,0:T(8,128)}, u32[]{:S(2)}) copy-start(f32[512,8192]{1,0:T(8,128)} %get-tuple-element.11) | copy-start | bytes 50331652
  634.7 36.8 %slice-start.4 = ((s8[16777216]{0:T(1024)(128)(4,1)}), s8[4194304]{0:T(1024)(128)(4,1)S(1)}, s32[]{:S(2)}) async-start(s8[16777216]{0:T(1024)(128)(4,1)} %bitcast.55), calls=%async_computation.6 | async-start | bytes 8388608
  634.7 36.8 %slice-start.5 = ((s8[16777216]{0:T(1024)(128)(4,1)}), s8[4194304]{0:T(1024)(128)(4,1)S(1)}, s32[]{:S(2)}) async-start(s8[16777216]{0:T(1024)(128)(4,1)} %bitcast.55), calls=%async_computation.7 | async-start | bytes 8388608
  652.9 18.6 %slice-start.6 = ((s8[16777216]{0:T(1024)(128)(4,1)}), s8[4194304]{0:T(1024)(128)(4,1)S(1)}, s32[]{:S(2)}) async-start(s8[16777216]{0:T(1024)(128)(4,1)} %bitcast.55), calls=%async_computation.8 | async-start | bytes 8388608
  652.9 18.6 %slice-start.7 = ((s8[16777216]{0:T(1024)(128)(4,1)}), s8[4194304]{0:T(1024)(128)(4,1)S(1)}, s32[]{:S(2)}) async-start(s8[16777216]{0:T(1024)(128)(4,1)} %bitcast.55), calls=%async_computation.9 | async-start | bytes 8388608
  691.2 36.6 %slice-start = ((s8[16777216]{0:T(1024)(128)(4,1)}), s8[4194304]{0:T(1024)(128)(4,1)S(1)}, s32[]{:S(2)}) async-start(s8[16777216]{0:T(1024)(128)(4,1)} %bitcast.53), calls=%async_computation.2 | async-start | bytes 8388608
  691.2 36.6 %slice-start.1 = ((s8[16777216]{0:T(1024)(128)(4,1)}), s8[4194304]{0:T(1024)(128)(4,1)S(1)}, s32[]{:S(2)}) async-start(s8[16777216]{0:T(1024)(128)(4,1)} %bitcast.53), calls=%async_computation.3 | async-start | bytes 8388608
  709.4 18.4 %slice-start.2 = ((s8[16777216]{0:T(1024)(128)(4,1)}), s8[4194304]{0:T(1024)(128)(4,1)S(1)}, s32[]{:S(2)}) async-start(s8[16777216]{0:T(1024)(128)(4,1)} %bitcast.53), calls=%async_computation.4 | async-start | bytes 8388608
  709.5 18.4 %slice-start.3 = ((s8[16777216]{0:T(1024)(128)(4,1)}), s8[4194304]{0:T(1024)(128)(4,1)S(1)}, s32[]{:S(2)}) async-start(s8[16777216]{0:T(1024)(128)(4,1)} %bitcast.53), calls=%async_computation.5 | async-start | bytes 8388608
Sparse Core Ops, SparseCore 0:
  31.8 505.7 all-gather.1
